TPU v7x, 512 devices: a whole 4x8x8 slice. The times are simulated.
512 devices in a mesh: dp: 2 (over core), pipe: 4 (over x), ctx: 64 (over z, y).
Axes of the slice: x: 4, y: 8, z: 8, core: 2. Of those that a mesh axis runs over, the one named last changes fastest.
Arguments:
- inputs: bfloat16 [4, 4096, 768], P('dp', 'ctx'), may hold values from -16 to 16
- cotangent: bfloat16 [4, 4096, 768], P('dp', 'ctx'), may hold values from -6 to 6
- dilated_kernel_weight: bfloat16 [4, 3, 768, 384], P('pipe'), may hold values from -0.125 to 0.125
- point_weight: bfloat16 [4, 384, 768], P('pipe'), may hold values from -0.3125 to 0.3125
Outputs:
- dilated_grad: float32 [4, 3, 768, 384], P('pipe', None, ('dp', 'ctx'))
All inputs are finite; a program needn't handle non-finite values.
Results may differ from a plain program's by a relative error of at most 0.012.
Values may be sent and summed in bfloat16 or wider, within the bound.
A program may use at most 64 MiB of HBM per device.

v0:
```python
import math

import jax
import jax.numpy as jnp
from jax import lax
from jax.sharding import PartitionSpec as P

root_half = 0.7071067811865476
inv_root_two_pi = 0.3989422804014327


def padded(cells, sides, width):
    for axis, dim in sides:
        count = lax.axis_size(axis)
        ends = count - 1
        head = lax.slice_in_dim(cells, 0, width, axis=dim)
        tail = lax.slice_in_dim(cells, cells.shape[dim] - width, cells.shape[dim], axis=dim)
        cells = jnp.concatenate(
            [
                lax.ppermute(tail, axis, [(i, (i + 1) % count) for i in range(ends)]),
                cells,
                lax.ppermute(head, axis, [((i + 1) % count, i) for i in range(ends)]),
            ],
            axis=dim,
        )
    return cells


def shifted(block, axis, distance):
    devices = range(lax.axis_size(axis))
    route = [(i - distance, i) for i in devices if i - distance in devices]
    return lax.ppermute(block, axis, route)


def gelu(value):
    return 0.5 * value * (1.0 + lax.erf(value * root_half))


def gelu_slope(value):
    return (
        0.5 * (1.0 + lax.erf(value * root_half))
        + value * jnp.exp(-0.5 * value * value) * inv_root_two_pi
    )


def shards(inputs, cotangent, dilated_kernel_weight, point_weight):
    sections = lax.axis_size("pipe")
    section = lax.axis_index("pipe")
    seq_count, bins, chans = inputs.shape
    reach = bins // 2
    table = jnp.array(
        [reach // 2 ** (sections - 1 - level) for level in range(sections)], jnp.int32
    )
    spread = table[section]
    dilation_weight = dilated_kernel_weight[0]
    w_point = point_weight[0]
    inner_channel_count = dilation_weight.shape[2]
    scale = 1.0 / math.sqrt(seq_count * lax.axis_size("dp") * bins * lax.axis_size("ctx"))
    ticks = jnp.arange(seq_count + sections - 1, dtype=jnp.int32)
    contract_final_axis = (((1,), (1,)), ((), ()))
    contract_first = (((0,), (0,)), ((), ()))

    def conv_fore(extended):
        running_total = jnp.zeros((bins, inner_channel_count), jnp.float32)
        for kernel_offset in range(3):
            receptive_span = lax.dynamic_slice_in_dim(
                extended, reach + (kernel_offset - 1) * spread, bins, 0
            )
            running_total = running_total + jnp.dot(
                receptive_span, dilation_weight[kernel_offset], preferred_element_type=jnp.float32
            )
        return running_total

    def put(store, slot, valid, item):
        current = lax.dynamic_index_in_dim(store, slot, 0, keepdims=False)
        return lax.dynamic_update_index_in_dim(store, jnp.where(valid, item, current), slot, 0)

    kept_x = jnp.zeros(inputs.shape, jnp.bfloat16)
    kept_ext = jnp.zeros((seq_count, bins + 2 * reach, chans), jnp.bfloat16)
    kept_pre = jnp.zeros((seq_count, bins, inner_channel_count), jnp.float32)

    def fore_tick(carry, tick):
        received, store_x, store_ext, store_pre = carry
        micro = tick - section
        valid = (micro >= 0) & (micro < seq_count)
        slot = jnp.clip(micro, 0, seq_count - 1)
        first = lax.dynamic_index_in_dim(inputs, slot, 0, keepdims=False)
        trunk_in = jnp.where(section == 0, first, received)
        act = gelu(trunk_in.astype(jnp.float32)).astype(jnp.bfloat16)
        extended = padded(act, (("ctx", 0),), reach)
        pre = conv_fore(extended)
        inner = gelu(pre).astype(jnp.bfloat16)
        out = (
            trunk_in.astype(jnp.float32)
            + jnp.dot(inner, w_point, preferred_element_type=jnp.float32)
        ).astype(jnp.bfloat16)
        sent = shifted(out, "pipe", 1)
        store_x = put(store_x, slot, valid, trunk_in)
        store_ext = put(store_ext, slot, valid, extended)
        store_pre = put(store_pre, slot, valid, pre)
        return ((sent, store_x, store_ext, store_pre), None)

    start_recv = jnp.zeros((bins, chans), jnp.bfloat16)
    (unused, kept_x, kept_ext, kept_pre), unused_out = lax.scan(
        fore_tick, (start_recv, kept_x, kept_ext, kept_pre), ticks
    )

    def back_tick(carry, tick):
        received, grad = carry
        micro = tick - (sections - 1 - section)
        valid = (micro >= 0) & (micro < seq_count)
        slot = jnp.clip(micro, 0, seq_count - 1)
        last = (
            lax.dynamic_index_in_dim(cotangent, slot, 0, keepdims=False).astype(jnp.float32) * scale
        ).astype(jnp.bfloat16)
        upstream = jnp.where(section == sections - 1, last, received)
        trunk_in = lax.dynamic_index_in_dim(kept_x, slot, 0, keepdims=False)
        extended = lax.dynamic_index_in_dim(kept_ext, slot, 0, keepdims=False)
        pre = lax.dynamic_index_in_dim(kept_pre, slot, 0, keepdims=False)
        inner_grad = lax.dot_general(
            upstream, w_point, contract_final_axis, preferred_element_type=jnp.float32
        )
        dpre = (inner_grad * gelu_slope(pre) * valid.astype(jnp.float32)).astype(jnp.bfloat16)
        dpre_ext = padded(dpre, (("ctx", 0),), reach)
        dact = jnp.zeros((bins, chans), jnp.float32)
        taps = []
        for kernel_offset in range(3):
            receptive_span = lax.dynamic_slice_in_dim(
                dpre_ext, reach - (kernel_offset - 1) * spread, bins, 0
            )
            dact = dact + lax.dot_general(
                receptive_span,
                dilation_weight[kernel_offset],
                contract_final_axis,
                preferred_element_type=jnp.float32,
            )
            source = lax.dynamic_slice_in_dim(
                extended, reach + (kernel_offset - 1) * spread, bins, 0
            )
            taps.append(
                lax.dot_general(source, dpre, contract_first, preferred_element_type=jnp.float32)
            )
        grad = grad + jnp.stack(taps)
        back = (
            upstream.astype(jnp.float32) + dact * gelu_slope(trunk_in.astype(jnp.float32))
        ).astype(jnp.bfloat16)
        sent = shifted(back, "pipe", -1)
        return ((sent, grad), None)

    start_grad = jnp.zeros((3, chans, inner_channel_count), jnp.float32)
    (unused_back, grad), unused_seq = lax.scan(back_tick, (start_recv, start_grad), ticks)
    term = grad[None]
    return lax.psum_scatter(term, ("dp", "ctx"), scatter_dimension=2, tiled=True)


def solution(mesh):
    return jax.shard_map(
        shards,
        mesh=mesh,
        in_specs=(
            P("dp", "ctx", None),
            P("dp", "ctx", None),
            P("pipe", None, None, None),
            P("pipe", None, None),
        ),
        out_specs=P("pipe", None, ("dp", "ctx"), None),
        check_vma=False,
    )
```

profile of v0, /device:TPU:24, one launch (start us, length us, event | category | flops | bytes accessed | tf_op | source)
XLA Modules:
  0.0 549.3 jit_solution(3093450169036282856)
XLA Ops:
  14.1 135.0 %while.35 = (s32[]{:T(128)}, bf16[64,768]{1,0:T(8,128)(2,1)}, bf16[2,64,768]{2,1,0:T(8,128)(2,1)}, bf16[2,128,768]{2,1,0:T(8,128)(2,1)}, f32[2,64,384]{2,1,0:T(8...) while((s32[]{:T(128)}, bf16[64,768]{1,0:T(8,128)(2,1)}, ...), condition=%wide.region_1.2_spmd, body=%wide.region_0.1_spmd.sunk | while | flops 153305088 | bytes 15140965 | solution.py:104
  19.2 2.3 collective-permute-start
  21.6 4.7 collective-permute-start.1
  34.1 3.4 collective-permute-start.2
  47.7 4.8 collective-permute-start.1
  60.4 4.4 collective-permute-start.2
  74.7 5.1 collective-permute-start.1
  87.6 4.4 collective-permute-start.2
  101.8 5.1 collective-permute-start.1
  114.7 4.4 collective-permute-start.2
  128.9 5.1 collective-permute-start.1
  141.9 4.4 collective-permute-start.2
  149.7 157.2 %while.36 = (s32[]{:T(128)}, bf16[64,768]{1,0:T(8,128)(2,1)}, f32[3,768,384]{2,1,0:T(8,128)S(1)}, pred[]{:T(512)}, s32[5]{0:T(128)S(1)}, /*index=5*/s32[]{:T(128...) while((s32[]{:T(128)}, bf16[64,768]{1,0:T(8,128)(2,1)}, ...), condition=%wide.region_3.4_spmd.clone, body=%wide.region_2.3_spmd.clone.sunk | while | flops 269475840 | bytes 29348896 | solution.py:151
  155.6 5.1 collective-permute-start.4
  175.6 2.5 maximum_add_fusion.2
  178.1 3.4 collective-permute-done.5
  187.4 5.1 collective-permute-start.4
  207.3 2.5 maximum_add_fusion.2
  209.8 3.0 collective-permute-done.5
  218.8 5.1 collective-permute-start.4
  228.3 2.3 convolution_bitcast_fusion.6
  238.7 2.5 maximum_add_fusion.2
  241.2 3.0 collective-permute-done.5
  250.1 5.1 collective-permute-start.4
  259.6 2.3 convolution_bitcast_fusion.6
  270.1 2.5 maximum_add_fusion.2
  272.6 3.0 collective-permute-done.5
  281.5 5.1 collective-permute-start.4
  301.5 2.5 maximum_add_fusion.2
  303.9 3.0 collective-permute-done.5
  307.0 4.6 copy.9
  313.5 227.5 %all-reduce.3.cloned.1.call-done = f32[1,3,768,384]{3,1,0,2:T(4,128)} async-done(((f32[1,3,768,384]{3,1,0,2:T(4,128)}), f32[1,3,768,384]{3,1,0,2:T(4,128)}) %all-reduce.3.cloned.1.call-update) | async-done | bytes 3538960
  (296 shorter events, 186.1 us)
Async XLA Ops:
  6.5 534.5 %all-reduce.3.cloned.1.call-start = ((), (), s32[]{:S(2)}) async-start(), calls=%async_computation | async-start | bytes 9437184
  19.2 10.3 %collective-permute-start = (bf16[32,768]{1,0:T(8,128)(2,1)}, bf16[32,768]{1,0:T(8,128)(2,1)}, u32[]{:S(2)}, u32[]{:S(2)}) collective-permute-start(bf16[32,768]{1,0:T(8,128)(2,1)} %get-tuple-element.767), channel_id=1, source_target_pairs={{1,0},{2,1},{3,2},{4,3},{5,4},{6,5},{7,6},{8,7},{9,8},{10,9},{11,1... | collective-permute-start | bytes 147464 | tf_op jit(solution)/shard_map/while/body/eval_jaxpr/ppermute | solution.py:22
  21.6 8.0 %collective-permute-start.1 = (bf16[32,768]{1,0:T(8,128)(2,1)}, bf16[32,768]{1,0:T(8,128)(2,1)}, u32[]{:S(2)}, u32[]{:S(2)}) collective-permute-start(bf16[32,768]{1,0:T(8,128)(2,1)} %get-tuple-element.768), channel_id=1, source_target_pairs={{0,1},{1,2},{2,3},{3,4},{4,5},{5,6},{6,7},{7,8},{8,9},{9,10},{10,1... | collective-permute-start | bytes 147464 | tf_op jit(solution)/shard_map/while/body/eval_jaxpr/ppermute | solution.py:20
  34.1 5.6 %collective-permute-start.2 = (bf16[64,768]{1,0:T(8,128)(2,1)S(1)}, bf16[64,768]{1,0:T(8,128)(2,1)S(1)}, u32[]{:S(2)}, u32[]{:S(2)}) collective-permute-start(bf16[64,768]{1,0:T(8,128)(2,1)S(1)} %fusion.117), channel_id=1, source_target_pairs={{0,64},{64,128},{128,192},{1,65},{65,129},{129,193},{2,66},{66,130... | collective-permute-start | bytes 294920 | tf_op jit(solution)/shard_map/while/body/eval_jaxpr/ppermute | solution.py:32
  43.1 12.1 %copy-start.12 = (f32[2,64,384]{2,1,0:T(8,128)S(1)}, f32[2,64,384]{2,1,0:T(8,128)}, u32[]{:S(2)}) copy-start(f32[2,64,384]{2,1,0:T(8,128)} %get-tuple-element.810) | copy-start | bytes 589828 | tf_op jit(solution)/shard_map/while
  45.5 10.3 %collective-permute-start = (bf16[32,768]{1,0:T(8,128)(2,1)}, bf16[32,768]{1,0:T(8,128)(2,1)}, u32[]{:S(2)}, u32[]{:S(2)}) collective-permute-start(bf16[32,768]{1,0:T(8,128)(2,1)} %get-tuple-element.767), channel_id=1, source_target_pairs={{1,0},{2,1},{3,2},{4,3},{5,4},{6,5},{7,6},{8,7},{9,8},{10,9},{11,1... | collective-permute-start | bytes 147464 | tf_op jit(solution)/shard_map/while/body/eval_jaxpr/ppermute | solution.py:22
  47.7 8.1 %collective-permute-start.1 = (bf16[32,768]{1,0:T(8,128)(2,1)}, bf16[32,768]{1,0:T(8,128)(2,1)}, u32[]{:S(2)}, u32[]{:S(2)}) collective-permute-start(bf16[32,768]{1,0:T(8,128)(2,1)} %get-tuple-element.768), channel_id=1, source_target_pairs={{0,1},{1,2},{2,3},{3,4},{4,5},{5,6},{6,7},{7,8},{8,9},{9,10},{10,1... | collective-permute-start | bytes 147464 | tf_op jit(solution)/shard_map/while/body/eval_jaxpr/ppermute | solution.py:20
  60.4 6.6 %collective-permute-start.2 = (bf16[64,768]{1,0:T(8,128)(2,1)S(1)}, bf16[64,768]{1,0:T(8,128)(2,1)S(1)}, u32[]{:S(2)}, u32[]{:S(2)}) collective-permute-start(bf16[64,768]{1,0:T(8,128)(2,1)S(1)} %fusion.117), channel_id=1, source_target_pairs={{0,64},{64,128},{128,192},{1,65},{65,129},{129,193},{2,66},{66,130... | collective-permute-start | bytes 294920 | tf_op jit(solution)/shard_map/while/body/eval_jaxpr/ppermute | solution.py:32
  72.7 10.3 %collective-permute-start = (bf16[32,768]{1,0:T(8,128)(2,1)}, bf16[32,768]{1,0:T(8,128)(2,1)}, u32[]{:S(2)}, u32[]{:S(2)}) collective-permute-start(bf16[32,768]{1,0:T(8,128)(2,1)} %get-tuple-element.767), channel_id=1, source_target_pairs={{1,0},{2,1},{3,2},{4,3},{5,4},{6,5},{7,6},{8,7},{9,8},{10,9},{11,1... | collective-permute-start | bytes 147464 | tf_op jit(solution)/shard_map/while/body/eval_jaxpr/ppermute | solution.py:22
  74.7 8.4 %collective-permute-start.1 = (bf16[32,768]{1,0:T(8,128)(2,1)}, bf16[32,768]{1,0:T(8,128)(2,1)}, u32[]{:S(2)}, u32[]{:S(2)}) collective-permute-start(bf16[32,768]{1,0:T(8,128)(2,1)} %get-tuple-element.768), channel_id=1, source_target_pairs={{0,1},{1,2},{2,3},{3,4},{4,5},{5,6},{6,7},{7,8},{8,9},{9,10},{10,1... | collective-permute-start | bytes 147464 | tf_op jit(solution)/shard_map/while/body/eval_jaxpr/ppermute | solution.py:20
  87.6 6.6 %collective-permute-start.2 = (bf16[64,768]{1,0:T(8,128)(2,1)S(1)}, bf16[64,768]{1,0:T(8,128)(2,1)S(1)}, u32[]{:S(2)}, u32[]{:S(2)}) collective-permute-start(bf16[64,768]{1,0:T(8,128)(2,1)S(1)} %fusion.117), channel_id=1, source_target_pairs={{0,64},{64,128},{128,192},{1,65},{65,129},{129,193},{2,66},{66,130... | collective-permute-start | bytes 294920 | tf_op jit(solution)/shard_map/while/body/eval_jaxpr/ppermute | solution.py:32
  99.8 10.3 %collective-permute-start = (bf16[32,768]{1,0:T(8,128)(2,1)}, bf16[32,768]{1,0:T(8,128)(2,1)}, u32[]{:S(2)}, u32[]{:S(2)}) collective-permute-start(bf16[32,768]{1,0:T(8,128)(2,1)} %get-tuple-element.767), channel_id=1, source_target_pairs={{1,0},{2,1},{3,2},{4,3},{5,4},{6,5},{7,6},{8,7},{9,8},{10,9},{11,1... | collective-permute-start | bytes 147464 | tf_op jit(solution)/shard_map/while/body/eval_jaxpr/ppermute | solution.py:22
  101.8 8.4 %collective-permute-start.1 = (bf16[32,768]{1,0:T(8,128)(2,1)}, bf16[32,768]{1,0:T(8,128)(2,1)}, u32[]{:S(2)}, u32[]{:S(2)}) collective-permute-start(bf16[32,768]{1,0:T(8,128)(2,1)} %get-tuple-element.768), channel_id=1, source_target_pairs={{0,1},{1,2},{2,3},{3,4},{4,5},{5,6},{6,7},{7,8},{8,9},{9,10},{10,1... | collective-permute-start | bytes 147464 | tf_op jit(solution)/shard_map/while/body/eval_jaxpr/ppermute | solution.py:20
  114.7 6.6 %collective-permute-start.2 = (bf16[64,768]{1,0:T(8,128)(2,1)S(1)}, bf16[64,768]{1,0:T(8,128)(2,1)S(1)}, u32[]{:S(2)}, u32[]{:S(2)}) collective-permute-start(bf16[64,768]{1,0:T(8,128)(2,1)S(1)} %fusion.117), channel_id=1, source_target_pairs={{0,64},{64,128},{128,192},{1,65},{65,129},{129,193},{2,66},{66,130... | collective-permute-start | bytes 294920 | tf_op jit(solution)/shard_map/while/body/eval_jaxpr/ppermute | solution.py:32
  127.0 10.3 %collective-permute-start = (bf16[32,768]{1,0:T(8,128)(2,1)}, bf16[32,768]{1,0:T(8,128)(2,1)}, u32[]{:S(2)}, u32[]{:S(2)}) collective-permute-start(bf16[32,768]{1,0:T(8,128)(2,1)} %get-tuple-element.767), channel_id=1, source_target_pairs={{1,0},{2,1},{3,2},{4,3},{5,4},{6,5},{7,6},{8,7},{9,8},{10,9},{11,1... | collective-permute-start | bytes 147464 | tf_op jit(solution)/shard_map/while/body/eval_jaxpr/ppermute | solution.py:22
  128.9 8.4 %collective-permute-start.1 = (bf16[32,768]{1,0:T(8,128)(2,1)}, bf16[32,768]{1,0:T(8,128)(2,1)}, u32[]{:S(2)}, u32[]{:S(2)}) collective-permute-start(bf16[32,768]{1,0:T(8,128)(2,1)} %get-tuple-element.768), channel_id=1, source_target_pairs={{0,1},{1,2},{2,3},{3,4},{4,5},{5,6},{6,7},{7,8},{8,9},{9,10},{10,1... | collective-permute-start | bytes 147464 | tf_op jit(solution)/shard_map/while/body/eval_jaxpr/ppermute | solution.py:20
  141.9 6.6 %collective-permute-start.2 = (bf16[64,768]{1,0:T(8,128)(2,1)S(1)}, bf16[64,768]{1,0:T(8,128)(2,1)S(1)}, u32[]{:S(2)}, u32[]{:S(2)}) collective-permute-start(bf16[64,768]{1,0:T(8,128)(2,1)S(1)} %fusion.117), channel_id=1, source_target_pairs={{0,64},{64,128},{128,192},{1,65},{65,129},{129,193},{2,66},{66,130... | collective-permute-start | bytes 294920 | tf_op jit(solution)/shard_map/while/body/eval_jaxpr/ppermute | solution.py:32
  153.7 16.0 %collective-permute-start.3 = (bf16[32,384]{1,0:T(8,128)(2,1)}, bf16[32,384]{1,0:T(8,128)(2,1)}, u32[]{:S(2)}, u32[]{:S(2)}) collective-permute-start(bf16[32,384]{1,0:T(8,128)(2,1)} %get-tuple-element.788), channel_id=1, source_target_pairs={{1,0},{2,1},{3,2},{4,3},{5,4},{6,5},{7,6},{8,7},{9,8},{10,9},{11,1... | collective-permute-start | bytes 73736 | tf_op jit(solution)/shard_map/while/body/eval_jaxpr/ppermute | solution.py:22
  155.6 14.1 %collective-permute-start.4 = (bf16[32,384]{1,0:T(8,128)(2,1)}, bf16[32,384]{1,0:T(8,128)(2,1)}, u32[]{:S(2)}, u32[]{:S(2)}) collective-permute-start(bf16[32,384]{1,0:T(8,128)(2,1)} %get-tuple-element.789), channel_id=1, source_target_pairs={{0,1},{1,2},{2,3},{3,4},{4,5},{5,6},{6,7},{7,8},{8,9},{9,10},{10,1... | collective-permute-start | bytes 73736 | tf_op jit(solution)/shard_map/while/body/eval_jaxpr/ppermute | solution.py:20
  174.3 7.2 %collective-permute-start.5 = (bf16[64,768]{1,0:T(8,128)(2,1)}, bf16[64,768]{1,0:T(8,128)(2,1)}, u32[]{:S(2)}, u32[]{:S(2)}) collective-permute-start(bf16[64,768]{1,0:T(8,128)(2,1)} %fusion.137), channel_id=1, source_target_pairs={{64,0},{128,64},{192,128},{65,1},{129,65},{193,129},{66,2},{130,66... | collective-permute-start | bytes 294920 | tf_op jit(solution)/shard_map/while/body/eval_jaxpr/ppermute | solution.py:32
  185.5 16.0 %collective-permute-start.3 = (bf16[32,384]{1,0:T(8,128)(2,1)}, bf16[32,384]{1,0:T(8,128)(2,1)}, u32[]{:S(2)}, u32[]{:S(2)}) collective-permute-start(bf16[32,384]{1,0:T(8,128)(2,1)} %get-tuple-element.788), channel_id=1, source_target_pairs={{1,0},{2,1},{3,2},{4,3},{5,4},{6,5},{7,6},{8,7},{9,8},{10,9},{11,1... | collective-permute-start | bytes 73736 | tf_op jit(solution)/shard_map/while/body/eval_jaxpr/ppermute | solution.py:22
  187.4 14.1 %collective-permute-start.4 = (bf16[32,384]{1,0:T(8,128)(2,1)}, bf16[32,384]{1,0:T(8,128)(2,1)}, u32[]{:S(2)}, u32[]{:S(2)}) collective-permute-start(bf16[32,384]{1,0:T(8,128)(2,1)} %get-tuple-element.789), channel_id=1, source_target_pairs={{0,1},{1,2},{2,3},{3,4},{4,5},{5,6},{6,7},{7,8},{8,9},{9,10},{10,1... | collective-permute-start | bytes 73736 | tf_op jit(solution)/shard_map/while/body/eval_jaxpr/ppermute | solution.py:20
  206.0 6.8 %collective-permute-start.5 = (bf16[64,768]{1,0:T(8,128)(2,1)}, bf16[64,768]{1,0:T(8,128)(2,1)}, u32[]{:S(2)}, u32[]{:S(2)}) collective-permute-start(bf16[64,768]{1,0:T(8,128)(2,1)} %fusion.137), channel_id=1, source_target_pairs={{64,0},{128,64},{192,128},{65,1},{129,65},{193,129},{66,2},{130,66... | collective-permute-start | bytes 294920 | tf_op jit(solution)/shard_map/while/body/eval_jaxpr/ppermute | solution.py:32
  216.8 16.0 %collective-permute-start.3 = (bf16[32,384]{1,0:T(8,128)(2,1)}, bf16[32,384]{1,0:T(8,128)(2,1)}, u32[]{:S(2)}, u32[]{:S(2)}) collective-permute-start(bf16[32,384]{1,0:T(8,128)(2,1)} %get-tuple-element.788), channel_id=1, source_target_pairs={{1,0},{2,1},{3,2},{4,3},{5,4},{6,5},{7,6},{8,7},{9,8},{10,9},{11,1... | collective-permute-start | bytes 73736 | tf_op jit(solution)/shard_map/while/body/eval_jaxpr/ppermute | solution.py:22
  218.8 14.1 %collective-permute-start.4 = (bf16[32,384]{1,0:T(8,128)(2,1)}, bf16[32,384]{1,0:T(8,128)(2,1)}, u32[]{:S(2)}, u32[]{:S(2)}) collective-permute-start(bf16[32,384]{1,0:T(8,128)(2,1)} %get-tuple-element.789), channel_id=1, source_target_pairs={{0,1},{1,2},{2,3},{3,4},{4,5},{5,6},{6,7},{7,8},{8,9},{9,10},{10,1... | collective-permute-start | bytes 73736 | tf_op jit(solution)/shard_map/while/body/eval_jaxpr/ppermute | solution.py:20
  237.4 6.8 %collective-permute-start.5 = (bf16[64,768]{1,0:T(8,128)(2,1)}, bf16[64,768]{1,0:T(8,128)(2,1)}, u32[]{:S(2)}, u32[]{:S(2)}) collective-permute-start(bf16[64,768]{1,0:T(8,128)(2,1)} %fusion.137), channel_id=1, source_target_pairs={{64,0},{128,64},{192,128},{65,1},{129,65},{193,129},{66,2},{130,66... | collective-permute-start | bytes 294920 | tf_op jit(solution)/shard_map/while/body/eval_jaxpr/ppermute | solution.py:32
  248.2 16.0 %collective-permute-start.3 = (bf16[32,384]{1,0:T(8,128)(2,1)}, bf16[32,384]{1,0:T(8,128)(2,1)}, u32[]{:S(2)}, u32[]{:S(2)}) collective-permute-start(bf16[32,384]{1,0:T(8,128)(2,1)} %get-tuple-element.788), channel_id=1, source_target_pairs={{1,0},{2,1},{3,2},{4,3},{5,4},{6,5},{7,6},{8,7},{9,8},{10,9},{11,1... | collective-permute-start | bytes 73736 | tf_op jit(solution)/shard_map/while/body/eval_jaxpr/ppermute | solution.py:22
  250.1 14.1 %collective-permute-start.4 = (bf16[32,384]{1,0:T(8,128)(2,1)}, bf16[32,384]{1,0:T(8,128)(2,1)}, u32[]{:S(2)}, u32[]{:S(2)}) collective-permute-start(bf16[32,384]{1,0:T(8,128)(2,1)} %get-tuple-element.789), channel_id=1, source_target_pairs={{0,1},{1,2},{2,3},{3,4},{4,5},{5,6},{6,7},{7,8},{8,9},{9,10},{10,1... | collective-permute-start | bytes 73736 | tf_op jit(solution)/shard_map/while/body/eval_jaxpr/ppermute | solution.py:20
  268.8 6.8 %collective-permute-start.5 = (bf16[64,768]{1,0:T(8,128)(2,1)}, bf16[64,768]{1,0:T(8,128)(2,1)}, u32[]{:S(2)}, u32[]{:S(2)}) collective-permute-start(bf16[64,768]{1,0:T(8,128)(2,1)} %fusion.137), channel_id=1, source_target_pairs={{64,0},{128,64},{192,128},{65,1},{129,65},{193,129},{66,2},{130,66... | collective-permute-start | bytes 294920 | tf_op jit(solution)/shard_map/while/body/eval_jaxpr/ppermute | solution.py:32
  279.6 16.0 %collective-permute-start.3 = (bf16[32,384]{1,0:T(8,128)(2,1)}, bf16[32,384]{1,0:T(8,128)(2,1)}, u32[]{:S(2)}, u32[]{:S(2)}) collective-permute-start(bf16[32,384]{1,0:T(8,128)(2,1)} %get-tuple-element.788), channel_id=1, source_target_pairs={{1,0},{2,1},{3,2},{4,3},{5,4},{6,5},{7,6},{8,7},{9,8},{10,9},{11,1... | collective-permute-start | bytes 73736 | tf_op jit(solution)/shard_map/while/body/eval_jaxpr/ppermute | solution.py:22
  281.5 14.1 %collective-permute-start.4 = (bf16[32,384]{1,0:T(8,128)(2,1)}, bf16[32,384]{1,0:T(8,128)(2,1)}, u32[]{:S(2)}, u32[]{:S(2)}) collective-permute-start(bf16[32,384]{1,0:T(8,128)(2,1)} %get-tuple-element.789), channel_id=1, source_target_pairs={{0,1},{1,2},{2,3},{3,4},{4,5},{5,6},{6,7},{7,8},{8,9},{9,10},{10,1... | collective-permute-start | bytes 73736 | tf_op jit(solution)/shard_map/while/body/eval_jaxpr/ppermute | solution.py:20
  300.1 6.8 %collective-permute-start.5 = (bf16[64,768]{1,0:T(8,128)(2,1)}, bf16[64,768]{1,0:T(8,128)(2,1)}, u32[]{:S(2)}, u32[]{:S(2)}) collective-permute-start(bf16[64,768]{1,0:T(8,128)(2,1)} %fusion.137), channel_id=1, source_target_pairs={{64,0},{128,64},{192,128},{65,1},{129,65},{193,129},{66,2},{130,66... | collective-permute-start | bytes 294920 | tf_op jit(solution)/shard_map/while/body/eval_jaxpr/ppermute | solution.py:32
  (64 other events, 354.7 us)
Sparse Core Ops, SparseCore 0:
  311.7 229.2 all-reduce.2
where the time goes:
time: 553 us; the launch traced here: 549 us
  waiting for transfers between devices  249 us (45%)
  starting transfers between devices  97.7 us (18%)
  matrix products  97 us (18%)
  local copies, waits for them, and re-layouts  41.6 us (8%)
  other arithmetic  38.7 us (7%)
  between operations  17.5 us (3%)
  loops' own time  7.28 us (1%)
    unnamed x2, waiting for transfers between devices  228 us
    ppermute x10, starting transfers between devices, padded(): lax.ppermute(tail, axis, [(i, (i + 1) % count) for i in range(ends)])  50.6 us
    dot_general x15, matrix products, back_tick(): lax.dot_general(source, dpre, contract_first, preferred_element_type=jnp....  34.1 us
    dot_general x15, matrix products, back_tick(): lax.dot_general(receptive_span, dilation_weight[kernel_offset], contract_...  28.3 us
    ppermute x10, starting transfers between devices, shifted(): return lax.ppermute(block, axis, route)  27.3 us
    dot_general x15, matrix products, conv_fore(): jnp.dot(receptive_span, dilation_weight[kernel_offset], preferred_element...  26 us
    ppermute x10, waiting for transfers between devices, shifted(): return lax.ppermute(block, axis, route)  21.8 us
    ppermute x10, starting transfers between devices, padded(): lax.ppermute(head, axis, [((i + 1) % count, i) for i in range(ends)])  19.9 us
  transfers between devices with their start and end apart: 31, of which 11 were waited for; matrix products, arithmetic and copies ran while one was open for 14% of the time, Pallas kernels for 0%

commit v1 on v0

v1 whole, which is shorter than its diff:
```python
import math

import jax
import jax.numpy as jnp
from jax import lax
from jax.experimental import pallas as pl
from jax.experimental.pallas import tpu as pltpu
from jax.sharding import PartitionSpec as P

MESH = pl.DeviceIdType.MESH
F32 = jnp.float32
BF16 = jnp.bfloat16
RING = 8
OWN = 64
LEFT = 128
ROWS = 320
PAD = 16
C = 768
B = 384
WROWS = 3072
QUARTER = 192
root_half = 0.7071067811865476
inv_root_two_pi = 0.3989422804014327
FORE = ((0, 320), (16, 288), (32, 256), (64, 192))
BACK = ((128, 64), (112, 96), (96, 128), (64, 192))
DILATION = (4, 8, 16, 32)


def gelu_and_slope(value):
    bell = jnp.exp(-0.5 * value * value)
    t = 1.0 / (1.0 + (0.3275911 * root_half) * jnp.abs(value))
    series = t * (
        0.127414796 + t * (-0.142248368 + t * (0.7107068705 + t * (-0.7265760135 + t * 0.5307027145)))
    )
    tail = series * bell
    phi = jnp.where(value >= 0.0, 1.0 - tail, tail)
    return value * phi, phi + value * bell * inv_root_two_pi


def remote(src, dst, send, recv, device):
    return pltpu.make_async_remote_copy(
        src_ref=src, dst_ref=dst, send_sem=send, recv_sem=recv, device_id=device, device_id_type=MESH
    )


def meet(devices):
    barrier = pltpu.get_barrier_semaphore()
    for device in devices:
        pl.semaphore_signal(barrier, inc=1, device_id=device, device_id_type=MESH)
    pl.semaphore_wait(barrier, len(devices))


def place():
    core = lax.axis_index("dp")
    pipe = lax.axis_index("pipe")
    ctx = lax.axis_index("ctx")
    return core, pipe, ctx, ctx // RING, ctx % RING


def at(core, pipe, ctx):
    return (core, pipe, ctx)


def on_torus(z, y):
    return ((z + RING) % RING) * RING + (y + RING) % RING


class Copies:
    def __init__(self, send, recv):
        self.send, self.recv, self.made, self.number = send, recv, {}, {}

    def start(self, name, src, dst, device):
        i = self.number.setdefault(name, len(self.number))
        copy = remote(src, dst, self.send.at[i], self.recv.at[i], device)
        copy.start()
        self.made[name] = copy

    def arrived(self, name, dst, device):
        i = self.number[name]
        remote(dst, dst, self.send.at[i], self.recv.at[i], device).wait_recv()

    def drain(self):
        for copy in self.made.values():
            copy.wait_send()


def gather_kernel(inp, cot, wd, wp, wg, xe, ce, local, send, recv):
    core, pipe, ctx, z, y = place()
    count = RING * RING
    ahead, behind = (pipe + 1) % 4, (pipe + 3) % 4
    other = (pipe + 2) % 4
    parity = (y + z) % 2
    near = [on_torus(z + 1, y), on_torus(z - 1, y), on_torus(z, y + 1), on_torus(z, y - 1)]
    partner = at(1 - core, pipe, ctx)
    up, down = at(core, ahead, ctx), at(core, behind, ctx)
    beside = [at(core, pipe, n) for n in near]
    side = {o: at(core, pipe, (ctx + o + count) % count) for o in (1, -1, 2, -2)}

    loads = [pltpu.make_async_copy(wd.at[0, k], wg.at[pipe, pl.ds(k * C, C), :], local.at[k]) for k in range(3)]
    for h in range(2):
        loads.append(
            pltpu.make_async_copy(
                wp.at[0, :, pl.ds(h * B, B)], wg.at[pipe, pl.ds(3 * C + h * B, B), :], local.at[3 + h]
            )
        )
    loads.append(pltpu.make_async_copy(inp, xe.at[:, pl.ds(LEFT, OWN), :], local.at[5]))
    loads.append(pltpu.make_async_copy(cot, ce.at[:, pl.ds(OWN, OWN), :], local.at[6]))
    for load in loads:
        load.start()
    meet([partner, up, down] + beside + list(side.values()))
    for load in loads:
        load.wait()

    mine = (core * 2 + parity) * (4 * QUARTER)
    theirs = (core * 2 + 1 - parity) * (4 * QUARTER)

    def piece(layer, base, n):
        return wg.at[layer, pl.ds(pl.multiple_of(base + n * QUARTER, QUARTER), QUARTER), :]

    copies = Copies(send, recv)
    for n in range(4):
        copies.start(("up", n), piece(pipe, mine, n), piece(pipe, mine, n), up)
        copies.start(("down", n), piece(pipe, mine, n), piece(pipe, mine, n), down)
    copies.start("i+1", inp, xe.at[:, pl.ds(OWN, OWN), :], side[1])
    copies.start("i-1", inp, xe.at[:, pl.ds(LEFT + OWN, OWN), :], side[-1])
    copies.start("c+1", cot.at[:, pl.ds(8, 56), :], ce.at[:, pl.ds(8, 56), :], side[1])
    copies.start("c-1", cot.at[:, pl.ds(0, 56), :], ce.at[:, pl.ds(2 * OWN, 56), :], side[-1])
    copies.start("i+2", inp.at[:, pl.ds(8, 56), :], xe.at[:, pl.ds(8, 56), :], side[2])
    copies.start("i-2", inp.at[:, pl.ds(0, 56), :], xe.at[:, pl.ds(4 * OWN, 56), :], side[-2])

    def spread(layer, tag, n):
        block = piece(layer, mine, n)
        copies.start((tag, "near", n), block, block, beside[n])
        copies.start((tag, "chip", n), block, block, partner)

    for n in range(4):
        copies.arrived(("up", n), piece(behind, mine, n), down)
        if n < 2:
            copies.start(("up2", n), piece(behind, mine, n), piece(behind, mine, n), up)
        spread(behind, "behind", n)
        copies.arrived(("down", n), piece(ahead, mine, n), up)
        if n >= 2:
            copies.start(("down2", n), piece(ahead, mine, n), piece(ahead, mine, n), down)
        spread(ahead, "ahead", n)
    for n in range(4):
        if n < 2:
            copies.arrived(("up2", n), piece(other, mine, n), down)
        else:
            copies.arrived(("down2", n), piece(other, mine, n), up)
        spread(other, "other", n)
    layers = (("behind", behind), ("ahead", ahead), ("other", other))
    for tag, layer in layers:
        for n in range(4):
            block = piece(layer, theirs, n)
            copies.arrived((tag, "near", n), block, beside[n])
            copies.start((tag, "far", n), block, block, partner)
    core_mine = ((1 - core) * 2 + parity) * (4 * QUARTER)
    core_theirs = ((1 - core) * 2 + 1 - parity) * (4 * QUARTER)
    for tag, layer in layers:
        for n in range(4):
            copies.arrived((tag, "chip", n), piece(layer, core_mine, n), partner)
            copies.arrived((tag, "far", n), piece(layer, core_theirs, n), partner)
    copies.arrived("i+1", xe.at[:, pl.ds(OWN, OWN), :], side[-1])
    copies.arrived("i-1", xe.at[:, pl.ds(LEFT + OWN, OWN), :], side[1])
    copies.arrived("c+1", ce.at[:, pl.ds(8, 56), :], side[-1])
    copies.arrived("c-1", ce.at[:, pl.ds(2 * OWN, 56), :], side[1])
    copies.arrived("i+2", xe.at[:, pl.ds(8, 56), :], side[-2])
    copies.arrived("i-2", xe.at[:, pl.ds(4 * OWN, 56), :], side[2])
    copies.drain()


def blocks(first, count, body):
    if count == 0:
        return

    def step(i, carry):
        for s in range(2):
            body(s, pl.multiple_of(first + i * 16, 16))
        return carry

    lax.fori_loop(0, count // 16, step, 0)


def compute_kernel(wg, xe, ce, act_out, dpre_out, xs, acts, pre, inner, slope_x, slope_pre, dy, dpre):
    pipe = lax.axis_index("pipe")
    ctx = lax.axis_index("ctx")
    last = RING * RING - 1

    def outside(ref, shift, low, high):
        for where, first, end in (
            (ctx == 0, low, LEFT),
            (ctx == 1, low, LEFT - OWN),
            (ctx == last, LEFT + OWN, high),
            (ctx == last - 1, LEFT + 2 * OWN, high),
        ):
            if first < end:

                @pl.when(where)
                def _(first=first, end=end):
                    ref[:, pl.ds(first + shift, end - first), :] = jnp.zeros(
                        (2, end - first, ref.shape[2]), ref.dtype
                    )

    def trunk(layer):
        return xe if layer == 0 else xs.at[layer - 1]

    for layer in range(4):
        first, count = FORE[layer]
        d = DILATION[layer]
        x = trunk(layer)
        act = acts.at[layer]
        low = max(first - 16 * pl.cdiv(d, 16), 0)
        high = min(first + count + 16 * pl.cdiv(d, 16), ROWS)

        def plain(s, row):
            value, _ = gelu_and_slope(x[s, pl.ds(row, 16), :].astype(F32))
            act[s, pl.ds(row + PAD, 16), :] = value.astype(BF16)

        if layer > 0:
            keep, kept = BACK[layer - 1]

            def both(s, row):
                value, slope = gelu_and_slope(x[s, pl.ds(row, 16), :].astype(F32))
                act[s, pl.ds(row + PAD, 16), :] = value.astype(BF16)
                slope_x[layer - 1, s, pl.ds(row - 96, 16), :] = slope

            blocks(low, keep - low, plain)
            blocks(keep, kept, both)
            blocks(keep + kept, high - keep - kept, plain)
        else:
            blocks(low, high - low, plain)
        outside(act, PAD, low, high)

        lhs = jnp.concatenate(
            [
                jnp.concatenate(
                    [act[s, pl.ds(first + PAD + (k - 1) * d, count), :] for s in range(2)], axis=0
                )
                for k in range(3)
            ],
            axis=1,
        )
        total = jnp.dot(lhs, wg[layer, pl.ds(0, 3 * C), :], preferred_element_type=F32)
        for s in range(2):
            pre[s, pl.ds(first, count), :] = total[s * count : (s + 1) * count]

        keep, kept = BACK[layer]

        def inner_plain(s, row):
            value, _ = gelu_and_slope(pre[s, pl.ds(row, 16), :])
            inner[s, pl.ds(row, 16), :] = value.astype(BF16)

        def inner_both(s, row):
            value, slope = gelu_and_slope(pre[s, pl.ds(row, 16), :])
            inner[s, pl.ds(row, 16), :] = value.astype(BF16)
            slope_pre[layer, s, pl.ds(row - 64, 16), :] = slope

        blocks(first, keep - first, inner_plain)
        blocks(keep, kept, inner_both)
        blocks(keep + kept, first + count - keep - kept, inner_plain)
        if layer < 3:
            follow = xs.at[layer]
            left = jnp.concatenate([inner[s, pl.ds(first, count), :] for s in range(2)], axis=0)
            for h in range(2):
                product = jnp.dot(left, wg[layer, pl.ds(3 * C + h * B, B), :], preferred_element_type=F32)
                for s in range(2):
                    old = x[s, pl.ds(first, count), pl.ds(h * B, B)].astype(F32)
                    follow[s, pl.ds(first, count), pl.ds(h * B, B)] = (
                        old + product[s * count : (s + 1) * count]
                    ).astype(BF16)

    scale = 1.0 / math.sqrt(4 * 4096)
    transposed = (((1,), (1,)), ((), ()))
    dy[:, pl.ds(64, 192), :] = (ce[...].astype(F32) * scale).astype(BF16)
    for layer in (3, 2, 1, 0):
        first, count = BACK[layer]
        d = DILATION[layer]
        upstream = jnp.concatenate([dy[s, pl.ds(first, count), :] for s in range(2)], axis=0)
        inner_grad = lax.dot_general(
            upstream[:, :B], wg[layer, pl.ds(3 * C, B), :], transposed, preferred_element_type=F32
        ) + lax.dot_general(
            upstream[:, B:], wg[layer, pl.ds(3 * C + B, B), :], transposed, preferred_element_type=F32
        )
        for s in range(2):
            slope = slope_pre[layer, s, pl.ds(first - 64, count), :]
            dpre[s, pl.ds(first, count), :] = (inner_grad[s * count : (s + 1) * count] * slope).astype(BF16)
        outside(dpre, 0, first, first + count)

        @pl.when(pipe == layer)
        def _():
            for s in range(2):
                dpre_out[pl.ds(s * OWN, OWN), :] = dpre[s, pl.ds(LEFT, OWN), :]
                for k in range(3):
                    act_out[k, pl.ds(s * OWN, OWN), :] = acts[
                        layer, s, pl.ds(LEFT + PAD + (k - 1) * d, OWN), :
                    ]

        if layer > 0:
            first, count = BACK[layer - 1]
            total = None
            for k in range(3):
                left = jnp.concatenate(
                    [dpre[s, pl.ds(first - (k - 1) * d, count), :] for s in range(2)], axis=0
                )
                product = lax.dot_general(
                    left, wg[layer, pl.ds(k * C, C), :], transposed, preferred_element_type=F32
                )
                total = product if total is None else total + product
            for s in range(2):
                slope = slope_x[layer - 1, s, pl.ds(first - 96, count), :]
                old = dy[s, pl.ds(first, count), :].astype(F32)
                dy[s, pl.ds(first, count), :] = (old + total[s * count : (s + 1) * count] * slope).astype(BF16)


def reduce_kernel(act, dpre, out, ract, rdpre, g, zs, zr, gz, ys, yr, send, recv):
    core, pipe, ctx, z, y = place()
    partner = at(1 - core, pipe, ctx)
    up = at(core, pipe, on_torus(z + 1, y))
    down = at(core, pipe, on_torus(z - 1, y))
    row = {o: at(core, pipe, on_torus(z, y + o)) for o in range(1, RING)}
    meet([partner, up, down] + list(row.values()))

    def half(which):
        return pl.ds(pl.multiple_of(which * B, B), B)

    copies = Copies(send, recv)
    copies.start("dpre", dpre, rdpre, partner)
    copies.start("act", act.at[:, :, half(1 - core)], ract, partner)
    over_rows = (((0,), (0,)), ((), ()))
    for k in range(3):
        g[k] = lax.dot_general(act[k, :, half(core)], dpre[...], over_rows, preferred_element_type=F32)
    copies.arrived("dpre", rdpre, partner)
    copies.arrived("act", ract, partner)
    for k in range(3):
        g[k] += lax.dot_general(ract[k], rdpre[...], over_rows, preferred_element_type=F32)

    deep = B // RING

    def part(k, offset):
        target = (z + offset + RING) % RING
        return g[k, pl.ds(pl.multiple_of(target * deep, 16), deep), :]

    routes = [("up", up, down, 0, [4, 3, 2, 1]), ("down", down, up, 4, [-3, -2, -1])]
    for step in range(4):
        for name, device, source, base, offsets in routes:
            if step >= len(offsets):
                continue
            slot = base + step
            for k in range(3):
                value = part(k, offsets[step])
                if step > 0:
                    copies.arrived((name, step - 1, k), zr.at[slot - 1, k], source)
                    value = value + zr[slot - 1, k].astype(F32)
                zs[slot, k] = value.astype(BF16)
                copies.start((name, step, k), zs.at[slot, k], zr.at[slot, k], device)
    for k in range(3):
        copies.arrived(("up", 3, k), zr.at[3, k], down)
        copies.arrived(("down", 2, k), zr.at[6, k], up)
        gz[k] = part(k, 0) + zr[3, k].astype(F32) + zr[6, k].astype(F32)

    small = deep // RING
    for j in range(RING):
        for k in range(3):
            ys[j, k, pl.ds(0, small), :] = gz[k, pl.ds(j * small, small), :]
            ys[j, k, pl.ds(small, 2), :] = jnp.zeros((2, B), F32)
    for o in range(1, RING):
        copies.start(("row", o), ys.at[(y + o) % RING], yr.at[o], row[o])
    total = ys[y]
    for o in range(1, RING):
        copies.arrived(("row", o), yr.at[o], row[RING - o])
        total = total + yr[o]
    out[0] = total[:, :small, :]
    copies.drain()


def shards(inputs, cotangent, dilated_kernel_weight, point_weight):
    vmem = pl.BlockSpec(memory_space=pltpu.VMEM)
    anywhere = pl.BlockSpec(memory_space=pl.ANY)
    limit = 60 * 2**20
    wg, xe, ce = pl.pallas_call(
        gather_kernel,
        name="gather",
        out_shape=(
            jax.ShapeDtypeStruct((4, WROWS, B), BF16),
            jax.ShapeDtypeStruct((2, ROWS, C), BF16),
            jax.ShapeDtypeStruct((2, 3 * OWN, C), BF16),
        ),
        in_specs=[anywhere] * 4,
        out_specs=(vmem,) * 3,
        scratch_shapes=[
            pltpu.SemaphoreType.DMA((7,)),
            pltpu.SemaphoreType.DMA((64,)),
            pltpu.SemaphoreType.DMA((64,)),
        ],
        compiler_params=pltpu.CompilerParams(collective_id=0, has_side_effects=True, vmem_limit_bytes=limit),
    )(inputs, cotangent, dilated_kernel_weight, point_weight)
    act, dpre = pl.pallas_call(
        compute_kernel,
        name="tower",
        out_shape=(
            jax.ShapeDtypeStruct((3, 2 * OWN, C), BF16),
            jax.ShapeDtypeStruct((2 * OWN, B), BF16),
        ),
        in_specs=[vmem] * 3,
        out_specs=(vmem,) * 2,
        scratch_shapes=[
            pltpu.VMEM((3, 2, ROWS, C), BF16),
            pltpu.VMEM((4, 2, ROWS + 2 * PAD, C), BF16),
            pltpu.VMEM((2, ROWS, B), F32),
            pltpu.VMEM((2, ROWS, B), BF16),
            pltpu.VMEM((3, 2, 128, C), F32),
            pltpu.VMEM((4, 2, 192, B), F32),
            pltpu.VMEM((2, ROWS, C), BF16),
            pltpu.VMEM((2, ROWS, B), BF16),
        ],
        compiler_params=pltpu.CompilerParams(vmem_limit_bytes=limit),
    )(wg, xe, ce)
    deep = B // RING
    return pl.pallas_call(
        reduce_kernel,
        name="reduce",
        out_shape=jax.ShapeDtypeStruct((1, 3, deep // RING, B), F32),
        in_specs=[vmem] * 2,
        out_specs=vmem,
        scratch_shapes=[
            pltpu.VMEM((3, 2 * OWN, B), BF16),
            pltpu.VMEM((2 * OWN, B), BF16),
            pltpu.VMEM((3, B, B), F32),
            pltpu.VMEM((7, 3, deep, B), BF16),
            pltpu.VMEM((7, 3, deep, B), BF16),
            pltpu.VMEM((3, deep, B), F32),
            pltpu.VMEM((RING, 3, 8, B), F32),
            pltpu.VMEM((RING, 3, 8, B), F32),
            pltpu.SemaphoreType.DMA((32,)),
            pltpu.SemaphoreType.DMA((32,)),
        ],
        compiler_params=pltpu.CompilerParams(collective_id=1, has_side_effects=True, vmem_limit_bytes=limit),
    )(act, dpre)


def solution(mesh):
    return jax.shard_map(
        shards,
        mesh=mesh,
        in_specs=(
            P("dp", "ctx", None),
            P("dp", "ctx", None),
            P("pipe", None, None, None),
            P("pipe", None, None),
        ),
        out_specs=P("pipe", None, ("dp", "ctx"), None),
        check_vma=False,
    )
```

time: 553 us -> 106 us (0.19)
  the two profiles are of different devices: /device:TPU:24 before, /device:TPU:16 now
where the time goes in v1:
time: 106 us
  Pallas kernels  104 us (98%)
  local copies, waits for them, and re-layouts  1.41 us (1%)
    pallas_call x1, Pallas kernels, shards(): pl.pallas_call(gather_kernel, name='gather', out_shape=(jax.ShapeDtypeStr...  45.2 us
    pallas_call x1, Pallas kernels, shards(): pl.pallas_call(reduce_kernel, name='reduce', out_shape=jax.ShapeDtypeStru...  31.4 us
    pallas_call x1, Pallas kernels, shards(): pl.pallas_call(compute_kernel, name='tower', out_shape=(jax.ShapeDtypeStr...  27.5 us

profile of v1, /device:TPU:16, one launch (start us, length us, event | category | flops | bytes accessed | tf_op | source)
XLA Modules:
  0.0 105.6 jit_solution(6993900704176883337)
XLA Ops:
  0.0 45.2 %gather.1 = (bf16[4,3072,384]{2,1,0:T(8,128)(2,1)}, bf16[2,320,768]{2,1,0:T(8,128)(2,1)}, bf16[2,192,768]{2,1,0:T(8,128)(2,1)}) custom-call(bf16[2,64,768]{2,1,0:T(8,128)(2,1)} %inp.1, bf16[2,64,768]{2,1,0:T(8,128)(2,1)} %cot.1, bf16[1,3,768,384]{3,2,1,0:T(8,128)(2,1)} %wd.1, bf16[1,384,768]{2,1,0:T(8,128)(2,1)} %wp.1), custom_call_target="tpu_custom_call" | custom-call | tf_op jit(solution)/shard_map/gather/pallas_call | solution.py:380
  45.3 27.5 %tower.1 = (bf16[3,128,768]{2,1,0:T(8,128)(2,1)}, bf16[128,384]{1,0:T(8,128)(2,1)}) custom-call(bf16[4,3072,384]{2,1,0:T(8,128)(2,1)} %get-tuple-element.10.wg, bf16[2,320,768]{2,1,0:T(8,128)(2,1)} %get-tuple-element.11.xe, bf16[2,192,768]{2,1,0:T(8,128)(2,1)} %get-tuple-element.12.ce), custom_call_target="tpu_custom_call" | custom-call | tf_op jit(solution)/shard_map/tower/pallas_call | solution.py:397
  72.8 31.4 %reduce.1 = f32[1,3,6,384]{3,2,1,0:T(8,128)} custom-call(bf16[3,128,768]{2,1,0:T(8,128)(2,1)} %get-tuple-element.13.act, bf16[128,384]{1,0:T(8,128)(2,1)} %get-tuple-element.14.dpre), custom_call_target="tpu_custom_call" | custom-call | tf_op jit(solution)/shard_map/reduce/pallas_call | solution.py:419
  104.2 1.4 %copy.5 = f32[1,3,6,384]{3,0,2,1:T(1,128)} copy(f32[1,3,6,384]{3,2,1,0:T(8,128)} %reduce.1) | data formatting | bytes 55296 | tf_op jit(solution)/shard_map/reduce/pallas_call | solution.py:419
